TPU v7x, 32 devices: a whole 2x2x4 slice. The times are simulated.
32 devices in a mesh: slab: 8 (over z, y), subj: 2 (over core), tm: 2 (over x).
Axes of the slice: x: 2, y: 2, z: 4, core: 2. Of those that a mesh axis runs over, the one named last changes fastest.
Arguments:
- subject_data: bfloat16 [2, 16, 128, 2048], P('subj', 'slab', None, 'tm'), may hold values from -8 to 8
- template: bfloat16 [16, 128, 2048], P('slab', None, 'tm'), may hold values from -8 to 8
- neighbours: int32 [16, 27], P('slab'), may hold values from 0 to 15, as said below
- valid: int32 [16, 27], P('slab'), may hold values from 0 to 1, as said below
Outputs:
- new_template: bfloat16 [16, 128, 2048], P('slab', None, 'tm')
Inputs may be any that keep to these rules, and one draw needn't show every extreme that they name: `neighbours`: slots 9 l to 9 l + 8 of block b name blocks of the slab of b shifted by l - 1 (slabs hold 2 consecutive blocks); where that slab doesn't exist they name b itself. Slot 13 names b itself. `valid`: slot 13 is always 1; slots whose slab doesn't exist are 0.
All inputs are finite; a program needn't handle non-finite values.
Results may differ from a plain program's by a relative error of at most 0.007.
Values may be sent and summed in bfloat16 or wider, within the bound.
No kernel may reach another device: no remote copies, remote signals or barrier semaphores. Data moves between devices by JAX's collectives and lax.ppermute only.
A program may use at most 64 MiB of HBM per device.

v0:
```python
import jax
import jax.numpy as jnp
from jax import lax
from jax.sharding import PartitionSpec as P

ITERS = 3


def with_halo(cells, sides, width):
    for axis, dim in sides:
        count = lax.axis_size(axis)
        ends = count - 1
        head = lax.slice_in_dim(cells, 0, width, axis=dim)
        tail = lax.slice_in_dim(cells, cells.shape[dim] - width, cells.shape[dim], axis=dim)
        cells = jnp.concatenate(
            [
                lax.ppermute(tail, axis, [(i, (i + 1) % count) for i in range(ends)]),
                cells,
                lax.ppermute(head, axis, [((i + 1) % count, i) for i in range(ends)]),
            ],
            axis=dim,
        )
    return cells


def balance(cross, row_norm, col_norm, mask):
    width = cross.shape[-1]
    logits = cross * row_norm[None, :, None, None] * col_norm[:, None, :, :] / 0.03
    masked = mask[None, None, :, None]
    kernel = jnp.exp(logits) * masked
    target = masked / (width * jnp.sum(mask))
    filler = 1.0 - masked
    col_weight = jnp.ones((cross.shape[0], 1, cross.shape[2], width), jnp.float32)
    for step in range(ITERS):
        row_weight = 1.0 / width / jnp.sum(kernel * col_weight, axis=(2, 3), keepdims=True)
        col_weight = target / (jnp.sum(kernel * row_weight, axis=1, keepdims=True) + filler)
    flow = kernel * col_weight
    return (flow / jnp.sum(flow, axis=(2, 3), keepdims=True)).astype(jnp.bfloat16)


def square_sum(values):
    return jnp.einsum("...t,...t->...", values, values, preferred_element_type=jnp.float32)


def slot_cross(tmpl_block, extended, slots):
    whole = jnp.einsum("it,sejt->siej", tmpl_block, extended, preferred_element_type=jnp.float32)
    return jnp.take(whole, slots, axis=2)


def project(plan, extended, slots):
    places = (slots[:, None] == jnp.arange(extended.shape[1], dtype=jnp.int32)[None, :]).astype(
        jnp.float32
    )
    folded = jnp.einsum(
        "sikj,ke->siej", plan.astype(jnp.float32), places, precision=lax.Precision.HIGHEST
    )
    upper = folded.astype(jnp.bfloat16)
    lower = (folded - upper.astype(jnp.float32)).astype(jnp.bfloat16)
    total = jnp.einsum("siej,sejt->it", upper, extended, preferred_element_type=jnp.float32)
    return total + jnp.einsum("siej,sejt->it", lower, extended, preferred_element_type=jnp.float32)


def subject_mean(moved, count):
    total = lax.psum(moved, "subj")
    return (total / count).astype(jnp.bfloat16)


def on_device(subject_data, template, neighbours, valid):
    blocks_here = template.shape[0]
    share = blocks_here // lax.axis_size("tm")
    subjects_all = subject_data.shape[0] * lax.axis_size("subj")
    offsets = neighbours - (lax.axis_index("slab") - 1) * blocks_here
    mask_all = valid.astype(jnp.float32)
    first = lax.axis_index("tm") * share
    my_offsets = lax.dynamic_slice_in_dim(offsets, first, share, 0)
    my_mask = lax.dynamic_slice_in_dim(mask_all, first, share, 0)
    full_time = lax.all_gather(subject_data, "tm", axis=3, tiled=True)
    extended = with_halo(full_time, (("slab", 1),), blocks_here)
    mine = lax.all_to_all(template, "tm", split_axis=0, concat_axis=2, tiled=True)
    col_norm = lax.rsqrt(square_sum(extended) + 1e-06)
    row_norm = lax.rsqrt(square_sum(mine) + 1e-06)

    def one_block(inputs):
        tmpl_block, scale_rows, slots, mask = inputs
        cross = slot_cross(tmpl_block, extended, slots)
        plan = balance(cross, scale_rows, jnp.take(col_norm, slots, axis=1), mask)
        return project(plan, extended, slots)

    moved = lax.map(one_block, (mine, row_norm, my_offsets, my_mask))
    averaged = subject_mean(moved, subjects_all)
    return lax.all_to_all(averaged, "tm", split_axis=2, concat_axis=0, tiled=True)


def solution(mesh):
    placed = (
        P("subj", "slab", None, "tm"),
        P("slab", None, "tm"),
        P("slab", None),
        P("slab", None),
    )
    return jax.shard_map(
        on_device, mesh=mesh, in_specs=placed, out_specs=P("slab", None, "tm"), check_vma=False
    )
```

profile of v0, /device:TPU:0, one launch (start us, length us, event | category | flops | bytes accessed | tf_op | source)
XLA Modules:
  0.0 159.5 jit_solution(255287246146315666)
XLA Ops:
  7.3 4.2 %all-to-all-start = ((bf16[2,128,1024]{2,1,0:T(8,128)(2,1)}), bf16[2,128,1024]{2,1,0:T(8,128)(2,1)S(1)}, u32[]{:S(2)}, u32[]{:S(2)}) async-start(bf16[2,128,1024]{2,1,0:T(8,128)(2,1)} %param.5), calls=%async_computation | async-start | bytes 1048576 | tf_op jit(solution)/shard_map/all_to_all | solution.py:79
  11.5 21.4 %all-gather.2.cloned.1.call-done = bf16[1,2,128,2048]{3,2,1,0:T(8,128)(2,1)} async-done(((bf16[1,2,128,1024]{3,2,1,0:T(8,128)(2,1)}), bf16[1,2,128,2048]{3,2,1,0:T(8,128)(2,1)}) %all-gather.2.cloned.1.call-update) | async-done | bytes 1048592 | tf_op jit(solution)/shard_map/all_gather | solution.py:77
  32.9 1.3 collective-permute-start.1
  34.2 5.5 %collective-permute-start = (bf16[1,2,128,2048]{3,2,1,0:T(8,128)(2,1)}, bf16[1,2,128,2048]{3,2,1,0:T(8,128)(2,1)}, u32[]{:S(2)}, u32[]{:S(2)}) collective-permute-start(bf16[1,2,128,2048]{3,2,1,0:T(8,128)(2,1)} %all-gather.2.cloned.1.call-done), channel_id=1, source_target_pairs={{0,4},{4,8},{8,12},{12,16},{16,20},{20,24},{24,28},{1,5},{5,9},{9,... | collective-permute-start | bytes 3145736 | tf_op jit(solution)/shard_map/ppermute | solution.py:17
  43.0 1.2 reshape.327
  44.5 15.2 %collective-permute-done.1 = bf16[1,2,128,2048]{3,2,1,0:T(8,128)(2,1)S(1)} collective-permute-done((bf16[1,2,128,2048]{3,2,1,0:T(8,128)(2,1)}, bf16[1,2,128,2048]{3,2,1,0:T(8,128)(2,1)S(1)}, u32[]{:S(2)}, u32[]{:S(2)}) %collective-permute-start.1) | collective-permute-done | bytes 1048608 | tf_op jit(solution)/shard_map/ppermute | solution.py:19
  59.7 22.5 %collective-permute-done = bf16[1,2,128,2048]{3,2,1,0:T(8,128)(2,1)} collective-permute-done((bf16[1,2,128,2048]{3,2,1,0:T(8,128)(2,1)}, bf16[1,2,128,2048]{3,2,1,0:T(8,128)(2,1)}, u32[]{:S(2)}, u32[]{:S(2)}) %collective-permute-start) | collective-permute-done | bytes 1048608 | tf_op jit(solution)/shard_map/ppermute | solution.py:17
  82.2 1.8 %fusion = f32[6,128]{1,0:T(8,128)S(1)} fusion(bf16[1,2,128,2048]{3,2,1,0:T(8,128)(2,1)S(1)} %collective-permute-done.1, bf16[1,2,128,2048]{3,2,1,0:T(8,128)(2,1)S(1)} %copy-done, bf16[1,2,128,2048]{3,2,1,0:T(8,128)(2,1)} %collective-permute-done), kind=kLoop, calls=%fused_computation.3 | loop fusion | flops 7863552 | bytes 3148800 | tf_op jit(solution)/shard_map/...t,...t->.../dot_general | solution.py:42
  84.6 2.3 %convolution_bitcast_fusion.3 = f32[128,6,128]{0,2,1:T(8,128)S(1)} fusion(bf16[128,2048,1]{1,0,2:T(8,128)(2,1)} %reshape.327, bf16[1,2,128,2048]{3,2,1,0:T(8,128)(2,1)S(1)} %collective-permute-done.1, bf16[1,2,128,2048]{3,2,1,0:T(8,128)(2,1)S(1)} %copy-done, bf16[1,2,128,2048]{3,2,1,0:T(8,128)(2,1)} %collective-permute-done), kind=kOutput, calls=%fused_computation.31 | convolution fusion | flops 405798912 | bytes 4063232 | tf_op jit(solution)/shard_map/while/body/eval_jaxpr/it,sejt->siej/dot_general | solution.py:46
  88.5 1.4 multiply_reduce_fusion.5
  90.0 1.3 multiply_reduce_fusion.4
  91.3 1.4 multiply_reduce_fusion.3
  92.8 1.3 multiply_reduce_fusion.2
  94.1 1.4 multiply_reduce_fusion.1
  95.6 1.3 multiply_reduce_fusion
  96.9 1.3 fusion.15
  98.3 1.3 copy.17
  99.9 2.8 %convolution_bitcast_fusion = f32[128,2048]{1,0:T(8,128)S(1)} fusion(bf16[128,6,128]{2,1,0:T(8,128)(2,1)S(1)} %get-tuple-element.32, bf16[1,2,128,2048]{3,2,1,0:T(8,128)(2,1)} %copy-done.2, bf16[1,2,128,2048]{3,2,1,0:T(8,128)(2,1)} %all-gather.2.cloned.1.call-done, bf16[1,2,128,2048]{3,2,1,0:T(8,128)(2,1)} %collective-permute-done), kind=kOutput, calls=%fused_computation.5 | convolution fusion | flops 405798912 | bytes 4390912 | tf_op jit(solution)/shard_map/while/body/eval_jaxpr/siej,sejt->it/dot_general | solution.py:60
  102.7 3.0 %fusion.2 = f32[1,128,2048]{2,1,0:T(8,128)} fusion(f32[128,2048]{1,0:T(8,128)S(1)} %convolution_bitcast_fusion, bf16[128,6,128]{2,1,0:T(8,128)(2,1)S(1)} %get-tuple-element.23, bf16[1,2,128,2048]{3,2,1,0:T(8,128)(2,1)S(1)} %copy-done.3, bf16[1,2,128,2048]{3,2,1,0:T(8,128)(2,1)S(1)} %copy-done.1, bf16[1,2,128,2048]{3,2,1,0:T(8,128)(2,1)} %collective-permute-done), kind=kOutput, calls=%fused_computation.8 | convolution fusion | flops 406061056 | bytes 5439488 | tf_op jit(solution)/shard_map/while/body/eval_jaxpr/siej,sejt->it/dot_general | solution.py:59
  105.7 19.7 %all-reduce.2.cloned.1.call-done = f32[1,128,2048]{2,1,0:T(8,128)} async-done(((f32[1,128,2048]{2,1,0:T(8,128)}), f32[1,128,2048]{2,1,0:T(8,128)}) %all-reduce.2.cloned.1.call-update) | async-done | bytes 1048592 | tf_op jit(solution)/shard_map/psum | solution.py:64
  125.4 1.3 multiply_convert_fusion
  128.0 11.7 %reduce.12 = bf16[2048,128]{1,0:T(8,128)(2,1)S(1)} reduce(bf16[2048,1,128]{2,1,0:T(2,128)(2,1)S(1)} %bitcast.110, bf16[]{:T(256)} %broadcast.450), dimensions={1}, to_apply=%bitcast.98.reduce_sub_computation | reduce | bytes 1048578
  139.9 11.2 %all_to_all.33 = bf16[2,2,65536]{2,1,0:T(2,128)(2,1)S(1)} all-to-all(bf16[2,2,65536]{2,1,0:T(2,128)(2,1)S(1)} %reshape.335), channel_id=1, replica_groups=mesh['slab'=8,'subj'=2,'tm'=2] {'tm'}, dimensions={0} | all-to-all | bytes 1048576 | tf_op jit(solution)/shard_map/all_to_all | solution.py:91
  151.7 1.0 copy.21
  (42 shorter events, 8.2 us)
Async XLA Ops:
  6.5 26.4 %all-gather.2.cloned.1.call-start = ((), (), s32[]{:S(2)}) async-start(), calls=%async_computation.2 | async-start | bytes 1572864 | tf_op jit(solution)/shard_map/all_gather | solution.py:77
  7.3 35.2 %all-to-all-start = ((bf16[2,128,1024]{2,1,0:T(8,128)(2,1)}), bf16[2,128,1024]{2,1,0:T(8,128)(2,1)S(1)}, u32[]{:S(2)}, u32[]{:S(2)}) async-start(bf16[2,128,1024]{2,1,0:T(8,128)(2,1)} %param.5), calls=%async_computation | async-start | bytes 1048576 | tf_op jit(solution)/shard_map/all_to_all | solution.py:79
  11.5 113.9 %all-reduce.2.cloned.1.call-start = ((), (), s32[]{:S(2)}) async-start(), calls=%async_computation.3 | async-start | bytes 2097152 | tf_op jit(solution)/shard_map/psum | solution.py:64
  32.9 26.8 %collective-permute-start.1 = (bf16[1,2,128,2048]{3,2,1,0:T(8,128)(2,1)}, bf16[1,2,128,2048]{3,2,1,0:T(8,128)(2,1)S(1)}, u32[]{:S(2)}, u32[]{:S(2)}) collective-permute-start(bf16[1,2,128,2048]{3,2,1,0:T(8,128)(2,1)} %all-gather.2.cloned.1.call-done), channel_id=1, source_target_pairs={{4,0},{8,4},{12,8},{16,12},{20,16},{24,20},{28,24},{5,1},{9,5},{13... | collective-permute-start | bytes 3145736 | tf_op jit(solution)/shard_map/ppermute | solution.py:19
  34.2 48.0 %collective-permute-start = (bf16[1,2,128,2048]{3,2,1,0:T(8,128)(2,1)}, bf16[1,2,128,2048]{3,2,1,0:T(8,128)(2,1)}, u32[]{:S(2)}, u32[]{:S(2)}) collective-permute-start(bf16[1,2,128,2048]{3,2,1,0:T(8,128)(2,1)} %all-gather.2.cloned.1.call-done), channel_id=1, source_target_pairs={{0,4},{4,8},{8,12},{12,16},{16,20},{20,24},{24,28},{1,5},{5,9},{9,... | collective-permute-start | bytes 3145736 | tf_op jit(solution)/shard_map/ppermute | solution.py:17
  42.5 39.7 %copy-start = (bf16[1,2,128,2048]{3,2,1,0:T(8,128)(2,1)S(1)}, bf16[1,2,128,2048]{3,2,1,0:T(8,128)(2,1)}, u32[]{:S(2)}) copy-start(bf16[1,2,128,2048]{3,2,1,0:T(8,128)(2,1)} %all-gather.2.cloned.1.call-done) | copy-start | bytes 3145732
  59.7 27.2 %copy-start.2 = (bf16[1,2,128,2048]{3,2,1,0:T(8,128)(2,1)}, bf16[1,2,128,2048]{3,2,1,0:T(8,128)(2,1)S(1)}, u32[]{:S(2)}) copy-start(bf16[1,2,128,2048]{3,2,1,0:T(8,128)(2,1)S(1)} %collective-permute-done.1) | copy-start | bytes 3145732
  99.9 2.8 %copy-start.1 = (bf16[1,2,128,2048]{3,2,1,0:T(8,128)(2,1)S(1)}, bf16[1,2,128,2048]{3,2,1,0:T(8,128)(2,1)}, u32[]{:S(2)}) copy-start(bf16[1,2,128,2048]{3,2,1,0:T(8,128)(2,1)} %all-gather.2.cloned.1.call-done) | copy-start | bytes 3145732
  99.9 2.8 %copy-start.3 = (bf16[1,2,128,2048]{3,2,1,0:T(8,128)(2,1)S(1)}, bf16[1,2,128,2048]{3,2,1,0:T(8,128)(2,1)}, u32[]{:S(2)}) copy-start(bf16[1,2,128,2048]{3,2,1,0:T(8,128)(2,1)} %copy-done.2) | copy-start | bytes 3145732
Sparse Core Ops, SparseCore 0:
  8.9 23.9 all-gather.1
  105.8 19.5 all-reduce.1
where the time goes:
time: 160 us
  waiting for transfers between devices  79.5 us (50%)
  other arithmetic  27.6 us (17%)
  between operations  14.3 us (9%)
  blocking collectives  11.2 us (7%)
  starting transfers between devices  11.1 us (7%)
  matrix products  8.34 us (5%)
  local copies, waits for them, and re-layouts  7.44 us (5%)
    ppermute x1, waiting for transfers between devices, with_halo(): lax.ppermute(tail, axis, [(i, (i + 1) % count) for i in range(ends)])  22.5 us
    all_gather x1, waiting for transfers between devices, on_device(): full_time = lax.all_gather(subject_data, 'tm', axis=3, tiled=True)  21.4 us
    psum x1, waiting for transfers between devices, subject_mean(): total = lax.psum(moved, 'subj')  19.7 us
    ppermute x1, waiting for transfers between devices, with_halo(): lax.ppermute(head, axis, [((i + 1) % count, i) for i in range(ends)])  15.2 us
    unnamed x1, other arithmetic  11.7 us
    all_to_all x1, blocking collectives, on_device(): lax.all_to_all(averaged, 'tm', split_axis=2, concat_axis=0, tiled=True)  11.2 us
    ppermute x1, starting transfers between devices, with_halo(): lax.ppermute(tail, axis, [(i, (i + 1) % count) for i in range(ends)])  5.54 us
    all_to_all x1, starting transfers between devices, on_device(): lax.all_to_all(template, 'tm', split_axis=0, concat_axis=2, tiled=True)  4.25 us
  transfers between devices with their start and end apart: 5, of which 4 were waited for; matrix products, arithmetic and copies ran while one was open for 3% of the time, Pallas kernels for 0%

commit v1 on v0

v1 whole, which is shorter than its diff:
```python
import functools

import jax
import jax.numpy as jnp
from jax import lax
from jax.experimental import pallas as pl
from jax.experimental.pallas import tpu as pltpu
from jax.sharding import PartitionSpec as P

ITERS = 3
PIECES = ((0, 1, 0, 8), (1, 1, 0, 4), (1, 1, 4, 4))


def cuts(blocks, times, eighths):
    parts = []
    for first, count, start, length in PIECES if eighths else ((0, blocks, 0, 8),):
        parts.append((first, count, start * times // 8, length * times // 8))
    return parts


def rows_dot(left, right):
    return lax.dot_general(
        left, right, (((1,), (1,)), ((), ())), preferred_element_type=jnp.float32
    )


def square_sums(values):
    square = values.astype(jnp.float32)
    square = square * square
    upper = square.astype(jnp.bfloat16)
    lower = (square - upper.astype(jnp.float32)).astype(jnp.bfloat16)
    ones = jnp.ones((8, values.shape[1]), jnp.bfloat16)
    return rows_dot(ones, upper) + rows_dot(ones, lower)


def two_terms(values):
    upper = values.astype(jnp.bfloat16)
    lower = (values - upper.astype(jnp.float32)).astype(jnp.bfloat16)
    return jnp.concatenate([upper, lower], axis=0)


def cross_body(parts, blocks, width, with_rows, tmpl_ref, *refs):
    pieces, (local_ref, send_ref) = refs[: len(parts)], refs[len(parts) :]
    rows = tmpl_ref.shape[0]
    sums = [None] * blocks
    norms = [None] * blocks
    for (first, count, start, length), piece in zip(parts, pieces):
        for m in range(count):
            data = piece[m * width : (m + 1) * width, :]
            part = rows_dot(tmpl_ref[:, start : start + length], data)
            norm = square_sums(data)
            b = first + m
            sums[b] = part if sums[b] is None else sums[b] + part
            norms[b] = norm if norms[b] is None else norms[b] + norm
    for b in range(blocks):
        lanes = slice(b * width, (b + 1) * width)
        local_ref[:rows, lanes] = sums[b]
        local_ref[rows : rows + 8, lanes] = norms[b]
        send_ref[:rows, lanes] = sums[b].astype(jnp.bfloat16)
        send_ref[rows : rows + 16, lanes] = two_terms(norms[b])
    if with_rows:
        norm = square_sums(tmpl_ref[...])
        local_ref[rows + 8 : rows + 16, :] = norm
        send_ref[rows + 16 : rows + 32, :] = two_terms(norm)


def cross_call(tmpl, pieces, parts, blocks, width, with_rows):
    rows, lanes = tmpl.shape[0], blocks * width
    extra = 2 if with_rows else 1
    return pl.pallas_call(
        functools.partial(cross_body, parts, blocks, width, with_rows),
        out_shape=(
            jax.ShapeDtypeStruct((rows + 8 * extra, lanes), jnp.float32),
            jax.ShapeDtypeStruct((rows + 16 * extra, lanes), jnp.bfloat16),
        ),
    )(tmpl, *pieces)


def plan_body(parts, blocks, width, n_others, count_ref, goal_ref, *refs):
    groups = 3
    refs = list(refs)
    take = lambda n: [refs.pop(0) for _ in range(n)]
    local = take(groups)
    received = [take(n_others) for _ in range(groups)]
    data = [take(len(p)) for p in parts]
    out_ref, kernel_ref, plan_ref = refs
    rows = blocks * width
    lanes = blocks * width

    def total_rows(group, start, sent):
        value = local[group][start : start + 8, :]
        for other in received[group]:
            value = value + other[sent : sent + 8, :].astype(jnp.float32)
            value = value + other[sent + 8 : sent + 16, :].astype(jnp.float32)
        return value

    row_scale = lax.rsqrt(total_rows(0, rows + 8, rows + 16) + 1e-06)
    row_scale = jnp.transpose(jnp.broadcast_to(row_scale[:1], (width, lanes)))
    for group in range(groups):
        col_scale = lax.rsqrt(total_rows(group, rows, rows) + 1e-06)[:1] / 0.03
        for b in range(blocks):
            own = slice(b * width, (b + 1) * width)
            for m in range(blocks):
                cols = slice(m * width, (m + 1) * width)
                cross = local[group][own, cols]
                for other in received[group]:
                    cross = cross + other[own, cols].astype(jnp.float32)
                e = group * blocks + m
                kernel_ref[own, e * width : (e + 1) * width] = jnp.exp(
                    cross * row_scale[own, :] * col_scale[:, cols]
                )
    members = groups * blocks

    def kernel(b, e):
        return kernel_ref[b * width : (b + 1) * width, e * width : (e + 1) * width]

    def row_sum(b, weight):
        total = kernel(b, 0) * weight[0]
        for e in range(1, members):
            total = total + kernel(b, e) * weight[e]
        return jnp.sum(total, axis=1, keepdims=True)

    weights = [
        [jnp.full((1, width), count_ref[b, e], jnp.float32) for e in range(members)]
        for b in range(blocks)
    ]
    for step in range(ITERS):
        row_weight = [1.0 / width / row_sum(b, weights[b]) for b in range(blocks)]
        weights = [
            [
                jnp.where(
                    count_ref[b, e] > 0.0,
                    (count_ref[b, e] * goal_ref[b])
                    / jnp.sum(kernel(b, e) * row_weight[b], axis=0, keepdims=True),
                    0.0,
                )
                for e in range(members)
            ]
            for b in range(blocks)
        ]
    for b in range(blocks):
        share = 1.0 / row_sum(b, weights[b])
        for e in range(members):
            plan_ref[b * width : (b + 1) * width, e * width : (e + 1) * width] = (
                kernel(b, e) * weights[b][e] * share
            ).astype(jnp.bfloat16)

    edges = {0, out_ref.shape[1]}
    for group in parts:
        for _, _, start, length in group:
            edges |= {start, start + length}
    edges = sorted(edges)
    for low, high in zip(edges, edges[1:]):
        total = None
        for group in range(groups):
            for (first, count, start, length), piece in zip(parts[group], data[group]):
                if start <= low and high <= start + length:
                    e = group * blocks + first
                    part = jnp.dot(
                        plan_ref[:, e * width : (e + count) * width],
                        piece[:, low - start : high - start],
                        preferred_element_type=jnp.float32,
                    )
                    total = part if total is None else total + part
        out_ref[:, low:high] = total.astype(out_ref.dtype)


def plan_call(counts, goal, local, received, data, parts, blocks, width):
    rows = blocks * width
    smem = pl.BlockSpec(memory_space=pltpu.SMEM)
    vmem = pl.BlockSpec(memory_space=pltpu.VMEM)
    arrays = [*local, *(r for group in received for r in group), *(d for g in data for d in g)]
    return pl.pallas_call(
        functools.partial(plan_body, parts, blocks, width, len(received[0])),
        out_shape=jax.ShapeDtypeStruct((rows, data[0][0].shape[1]), jnp.bfloat16),
        in_specs=[smem, smem] + [vmem] * len(arrays),
        out_specs=vmem,
        scratch_shapes=[
            pltpu.VMEM((rows, 3 * rows), jnp.float32),
            pltpu.VMEM((rows, 3 * rows), jnp.bfloat16),
        ],
    )(counts, goal, *arrays)


def others(value, axis):
    count = lax.axis_size(axis)
    return [
        lax.ppermute(value, axis, [(i, (i + shift) % count) for i in range(count)])
        for shift in range(1, count)
    ]


def on_device(subject_data, template, neighbours, valid):
    _, blocks, width, times = subject_data.shape
    slabs = lax.axis_size("slab")
    subjects = subject_data.shape[0] * lax.axis_size("subj")
    slab = lax.axis_index("slab")
    data = subject_data[0]
    tmpl = template.reshape(blocks * width, times)

    pairs = [(i, i ^ 1) for i in range(slabs)]
    onward = [(i, i + 2) for i in range(0, slabs - 2, 2)]
    onward += [(i, i - 2) for i in range(3, slabs, 2)]
    parts = cuts(blocks, times, True)
    whole = cuts(blocks, times, False)
    own = [data.reshape(blocks * width, times)]
    near, far = [], []
    for first, count, start, length in parts:
        piece = data[first : first + count, :, start : start + length]
        near.append(lax.ppermute(piece, "slab", pairs))
        far.append(lax.ppermute(near[-1], "slab", onward))
    flat = lambda pieces: [p.reshape(p.shape[0] * width, p.shape[2]) for p in pieces]
    near, far = flat(near), flat(far)

    ahead = 1 - 2 * (slab % 2)
    members = jnp.arange(blocks)
    places = jnp.concatenate(
        [(slab + step) * blocks + members for step in (0, ahead, -ahead)]
    )
    used = valid.astype(jnp.float32)
    hits = (neighbours[:, :, None] == places[None, None, :]).astype(jnp.float32)
    counts = jnp.sum(hits * used[:, :, None], axis=1)
    goal = 1.0 / (width * jnp.sum(used, axis=1))

    results = [
        cross_call(tmpl, pieces, cut, blocks, width, rows)
        for pieces, cut, rows in ((own, whole, True), (near, parts, False), (far, parts, False))
    ]
    local = [r[0] for r in results]
    received = [others(r[1], "tm") for r in results]
    moved = plan_call(
        counts, goal, local, received, [own, near, far], [whole, parts, parts], blocks, width
    )
    total = moved.astype(jnp.float32)
    for other in others(moved, "subj"):
        total = total + other.astype(jnp.float32)
    return (total / subjects).astype(jnp.bfloat16).reshape(template.shape)


def solution(mesh):
    placed = (
        P("subj", "slab", None, "tm"),
        P("slab", None, "tm"),
        P("slab", None),
        P("slab", None),
    )
    return jax.shard_map(
        on_device, mesh=mesh, in_specs=placed, out_specs=P("slab", None, "tm"), check_vma=False
    )
```

time: 160 us -> 46.1 us (0.29)
  waiting for transfers between devices: 79.5 us -> 6.89 us
  other arithmetic: 27.6 us -> 2.97 us
  between operations: 14.3 us -> 0.14 us
  Pallas kernels: 0 us -> 12.3 us
  blocking collectives: 11.2 us -> 0 us
  starting transfers between devices: 11.1 us -> 19.6 us
  matrix products: 8.34 us -> 0 us
  local copies, waits for them, and re-layouts: 7.44 us -> 3.78 us
    ppermute x2 -> x10, waiting for transfers between devices: 37.7 us -> 6.89 us  [the longest x4 6.23 us: others(): lax.ppermute(value, axis, [(i, (i + shift) % count) for i in range(count)])]
    all_gather x1 -> x0, waiting for transfers between devices: 21.4 us -> none  [on_device(): full_time = lax.all_gather(subject_data, 'tm', axis=3, tiled=True)]
    psum x1 -> x0, waiting for transfers between devices: 19.7 us -> none  [subject_mean(): total = lax.psum(moved, 'subj')]
    ppermute x2 -> x10, starting transfers between devices: 6.82 us -> 19.6 us  [the longest x3 10.9 us: on_device(): far.append(lax.ppermute(near[-1], 'slab', onward))]
    pallas_call x0 -> x4, Pallas kernels: none -> 12.3 us  [the longest x3 8.16 us: cross_call(): pl.pallas_call(functools.partial(cross_body, parts, blocks, width, with_r...]
    unnamed x1 -> x0, other arithmetic: 11.7 us -> none
    all_to_all x1 -> x0, blocking collectives: 11.2 us -> none  [on_device(): lax.all_to_all(averaged, 'tm', split_axis=2, concat_axis=0, tiled=True)]
    reduce_sum x8 -> x2, other arithmetic: 9.54 us -> 0.27 us  [the longest x1 0.15 us: on_device(): counts = jnp.sum(hits * used[:, :, None], axis=1)]
  transfers between devices with their start and end apart: 5 -> 10, of which waited for: 4 -> 3; matrix products, arithmetic and copies ran while one was open for 3% -> 4% of each run, Pallas kernels for 0% -> 18%
where the time goes in v1:
time: 46.1 us; the launch traced here: 45.7 us
  starting transfers between devices  19.6 us (43%)
  Pallas kernels  12.3 us (27%)
  waiting for transfers between devices  6.89 us (15%)
  local copies, waits for them, and re-layouts  3.78 us (8%)
  other arithmetic  2.97 us (6%)
    ppermute x3, starting transfers between devices, on_device(): far.append(lax.ppermute(near[-1], 'slab', onward))  10.9 us
    pallas_call x3, Pallas kernels, cross_call(): pl.pallas_call(functools.partial(cross_body, parts, blocks, width, with_r...  8.16 us
    ppermute x4, waiting for transfers between devices, others(): lax.ppermute(value, axis, [(i, (i + shift) % count) for i in range(count)])  6.23 us
    ppermute x3, starting transfers between devices, on_device(): near.append(lax.ppermute(piece, 'slab', pairs))  5.15 us
    pallas_call x1, Pallas kernels, plan_call(): pl.pallas_call(functools.partial(plan_body, parts, blocks, width, len(rec...  4.15 us
    ppermute x4, starting transfers between devices, others(): lax.ppermute(value, axis, [(i, (i + shift) % count) for i in range(count)])  3.52 us
    unnamed x24, local copies, waits for them, and re-layouts  2.04 us
    convert_element_type x1, other arithmetic, on_device(): return (total / subjects).astype(jnp.bfloat16).reshape(template.shape)  2.03 us
  transfers between devices with their start and end apart: 10, of which 3 were waited for; matrix products, arithmetic and copies ran while one was open for 4% of the time, Pallas kernels for 18%

profile of v1, /device:TPU:0, one launch (start us, length us, event | category | flops | bytes accessed | tf_op | source)
XLA Modules:
  0.0 45.7 jit_solution(8835465858284563143)
XLA Ops:
  0.0 1.0 %slice_bitcast_fusion = bf16[1,128,1024]{2,1,0:T(8,128)(2,1)S(1)} fusion(bf16[1,2,128,1024]{3,2,1,0:T(8,128)(2,1)} %param.4), kind=kLoop, calls=%fused_computation.1 | loop fusion | bytes 524288 | tf_op jit(solution)/shard_map/slice | solution.py:209
  1.0 3.1 %collective-permute-start = (bf16[1,128,1024]{2,1,0:T(8,128)(2,1)S(1)}, bf16[1,128,1024]{2,1,0:T(8,128)(2,1)S(1)}, u32[]{:S(2)}, u32[]{:S(2)}) collective-permute-start(bf16[1,128,1024]{2,1,0:T(8,128)(2,1)S(1)} %slice_bitcast_fusion), channel_id=1, source_target_pairs={{0,4},{4,0},{8,12},{12,8},{16,20},{20,16},{24,28},{28,24},{1,5},{5... | collective-permute-start | bytes 786440 | tf_op jit(solution)/shard_map/ppermute | solution.py:210
  4.2 2.0 %collective-permute-start.1 = (bf16[1,128,512]{2,1,0:T(8,128)(2,1)S(1)}, bf16[1,128,512]{2,1,0:T(8,128)(2,1)S(1)}, u32[]{:S(2)}, u32[]{:S(2)}) collective-permute-start(bf16[1,128,512]{2,1,0:T(8,128)(2,1)S(1)} %get-tuple-element.18), channel_id=1, source_target_pairs={{0,4},{4,0},{8,12},{12,8},{16,20},{20,16},{24,28},{28,24},{1,5},{5... | collective-permute-start | bytes 393224 | tf_op jit(solution)/shard_map/ppermute | solution.py:210
  6.2 2.9 %shard_map.46 = (f32[272,256]{1,0:T(8,128)}, bf16[288,256]{1,0:T(8,128)(2,1)}) custom-call(bf16[256,1024]{1,0:T(8,128)(2,1)} %bitcast.12, bf16[256,1024]{1,0:T(8,128)(2,1)} %bitcast.15), custom_call_target="tpu_custom_call" | custom-call | tf_op jit(solution)/shard_map/pallas_call | solution.py:70
  9.1 1.5 %collective-permute-start.6 = (bf16[288,256]{1,0:T(8,128)(2,1)}, bf16[288,256]{1,0:T(8,128)(2,1)S(1)}, u32[]{:S(2)}, u32[]{:S(2)}) collective-permute-start(bf16[288,256]{1,0:T(8,128)(2,1)} %get-tuple-element.14), channel_id=1, source_target_pairs={{0,1},{1,0},{2,3},{3,2},{4,5},{5,4},{6,7},{7,6},{8,9},{9,8},{10,11... | collective-permute-start | bytes 442376 | tf_op jit(solution)/shard_map/ppermute | solution.py:188
  10.6 0.6 %collective-permute-done = bf16[1,128,1024]{2,1,0:T(8,128)(2,1)S(1)} collective-permute-done((bf16[1,128,1024]{2,1,0:T(8,128)(2,1)S(1)}, bf16[1,128,1024]{2,1,0:T(8,128)(2,1)S(1)}, u32[]{:S(2)}, u32[]{:S(2)}) %collective-permute-start) | collective-permute-done | bytes 262176 | tf_op jit(solution)/shard_map/ppermute | solution.py:210
  11.3 4.0 %collective-permute-start.3 = (bf16[1,128,1024]{2,1,0:T(8,128)(2,1)S(1)}, bf16[1,128,1024]{2,1,0:T(8,128)(2,1)S(1)}, u32[]{:S(2)}, u32[]{:S(2)}) collective-permute-start(bf16[1,128,1024]{2,1,0:T(8,128)(2,1)S(1)} %collective-permute-done), channel_id=1, source_target_pairs={{0,8},{8,16},{16,24},{12,4},{20,12},{28,20},{1,9},{9,17},{17,25},{... | collective-permute-start | bytes 786440 | tf_op jit(solution)/shard_map/ppermute | solution.py:211
  15.3 0.6 %copy-done.10 = s32[2,27]{1,0:T(2,128)S(1)} copy-done((s32[2,27]{1,0:T(2,128)S(1)}, s32[2,27]{1,0:T(2,128)}, u32[]{:S(2)}) %copy-start.10) | copy-done | bytes 240
  16.0 3.5 %collective-permute-start.5 = (bf16[1,128,512]{2,1,0:T(8,128)(2,1)S(1)}, bf16[1,128,512]{2,1,0:T(8,128)(2,1)S(1)}, u32[]{:S(2)}, u32[]{:S(2)}) collective-permute-start(bf16[1,128,512]{2,1,0:T(8,128)(2,1)S(1)} %collective-permute-done.2), channel_id=1, source_target_pairs={{0,8},{8,16},{16,24},{12,4},{20,12},{28,20},{1,9},{9,17},{17,25},{... | collective-permute-start | bytes 393224 | tf_op jit(solution)/shard_map/ppermute | solution.py:211
  19.5 3.5 %collective-permute-start.4 = (bf16[1,128,512]{2,1,0:T(8,128)(2,1)S(1)}, bf16[1,128,512]{2,1,0:T(8,128)(2,1)S(1)}, u32[]{:S(2)}, u32[]{:S(2)}) collective-permute-start(bf16[1,128,512]{2,1,0:T(8,128)(2,1)S(1)} %collective-permute-done.1), channel_id=1, source_target_pairs={{0,8},{8,16},{16,24},{12,4},{20,12},{28,20},{1,9},{9,17},{17,25},{... | collective-permute-start | bytes 393224 | tf_op jit(solution)/shard_map/ppermute | solution.py:211
  23.0 0.2 fusion
  23.1 0.7 %copy.5.count_ref = f32[2,6]{1,0:T(2,128)} copy(f32[2,6]{0,1:T(8,128)S(1)} %fusion) | data formatting | bytes 96 | tf_op jit(solution)/shard_map/reduce_sum | solution.py:222
  23.8 0.1 convert_reduce_fusion
  23.9 2.6 %shard_map.47 = (f32[264,256]{1,0:T(8,128)}, bf16[272,256]{1,0:T(8,128)(2,1)}) custom-call(bf16[256,1024]{1,0:T(8,128)(2,1)} %bitcast.13, bf16[128,1024]{1,0:T(8,128)(2,1)} %bitcast.18, bf16[128,512]{1,0:T(8,128)(2,1)} %bitcast.24, bf16[128,512]{1,0:T(8,128)(2,1)} %bitcast.22), custom_call_target="tpu_custom_call" | custom-call | tf_op jit(solution)/shard_map/pallas_call | solution.py:70
  26.6 1.5 %collective-permute-start.7 = (bf16[272,256]{1,0:T(8,128)(2,1)}, bf16[272,256]{1,0:T(8,128)(2,1)S(1)}, u32[]{:S(2)}, u32[]{:S(2)}) collective-permute-start(bf16[272,256]{1,0:T(8,128)(2,1)} %get-tuple-element.15), channel_id=1, source_target_pairs={{0,1},{1,0},{2,3},{3,2},{4,5},{5,4},{6,7},{7,6},{8,9},{9,8},{10,11... | collective-permute-start | bytes 417800 | tf_op jit(solution)/shard_map/ppermute | solution.py:188
  28.1 0.6 %copy-done.5 = bf16[1,128,512]{2,1,0:T(8,128)(2,1)} copy-done((bf16[1,128,512]{2,1,0:T(8,128)(2,1)}, bf16[1,128,512]{2,1,0:T(8,128)(2,1)S(1)}, u32[]{:S(2)}) %copy-start.5) | copy-done | bytes 131096
  28.9 2.6 %shard_map.48 = (f32[264,256]{1,0:T(8,128)}, bf16[272,256]{1,0:T(8,128)(2,1)}) custom-call(bf16[256,1024]{1,0:T(8,128)(2,1)} %bitcast.14, bf16[128,1024]{1,0:T(8,128)(2,1)} %bitcast.20, bf16[128,512]{1,0:T(8,128)(2,1)} %bitcast.28, bf16[128,512]{1,0:T(8,128)(2,1)} %bitcast.26), custom_call_target="tpu_custom_call" | custom-call | tf_op jit(solution)/shard_map/pallas_call | solution.py:70
  31.5 0.5 %collective-permute-start.8 = (bf16[272,256]{1,0:T(8,128)(2,1)}, bf16[272,256]{1,0:T(8,128)(2,1)S(1)}, u32[]{:S(2)}, u32[]{:S(2)}) collective-permute-start(bf16[272,256]{1,0:T(8,128)(2,1)} %get-tuple-element.16), channel_id=1, source_target_pairs={{0,1},{1,0},{2,3},{3,2},{4,5},{5,4},{6,7},{7,6},{8,9},{9,8},{10,11... | collective-permute-start | bytes 417800 | tf_op jit(solution)/shard_map/ppermute | solution.py:188
  32.0 0.6 %multiply_divide_fusion.goal_ref = f32[2]{0:T(128)} fusion(f32[2]{0:T(128)S(1)} %convert_reduce_fusion), kind=kLoop, calls=%fused_computation.5 | loop fusion | flops 4 | bytes 16 | tf_op jit(solution)/shard_map/div | solution.py:223
  32.7 4.1 %collective-permute-done.8.refs_5_ = bf16[272,256]{1,0:T(8,128)(2,1)S(1)} collective-permute-done((bf16[272,256]{1,0:T(8,128)(2,1)}, bf16[272,256]{1,0:T(8,128)(2,1)S(1)}, u32[]{:S(2)}, u32[]{:S(2)}) %collective-permute-start.8) | collective-permute-done | bytes 139296 | tf_op jit(solution)/shard_map/ppermute | solution.py:188
  36.8 0.6 %copy-done.9 = bf16[272,256]{1,0:T(8,128)(2,1)} copy-done((bf16[272,256]{1,0:T(8,128)(2,1)}, bf16[272,256]{1,0:T(8,128)(2,1)S(1)}, u32[]{:S(2)}) %copy-start.9) | copy-done | bytes 139288
  37.4 4.2 %shard_map.49 = bf16[256,1024]{1,0:T(8,128)(2,1)} custom-call(f32[2,6]{1,0:T(2,128)} %copy.5.count_ref, f32[2]{0:T(128)} %multiply_divide_fusion.goal_ref, f32[272,256]{1,0:T(8,128)} %get-tuple-element.11.refs_0_, f32[264,256]{1,0:T(8,128)} %get-tuple-element.12.refs_1_, f32[264,256]{1,0:T(8,128)} %get-tuple-element.13.refs_2_, bf16[288,256]{1,0:T(8,128)(2,1)} %copy-done.7, ...), custom_call_target="tpu_custom_call" | custom-call | tf_op jit(solution)/shard_map/pallas_call | solution.py:173
  41.6 2.1 %collective-permute-done.9 = bf16[256,1024]{1,0:T(8,128)(2,1)S(1)} collective-permute-done((bf16[256,1024]{1,0:T(8,128)(2,1)}, bf16[256,1024]{1,0:T(8,128)(2,1)S(1)}, u32[]{:S(2)}, u32[]{:S(2)}) %collective-permute-start.9) | collective-permute-done | bytes 524320 | tf_op jit(solution)/shard_map/ppermute | solution.py:188
  43.7 2.0 %multiply_convert_fusion = bf16[256,1024]{1,0:T(8,128)(2,1)} fusion(bf16[256,1024]{1,0:T(8,128)(2,1)S(1)} %collective-permute-done.9, bf16[256,1024]{1,0:T(8,128)(2,1)} %shard_map.49), kind=kLoop, calls=%fused_computation | loop fusion | flops 1310720 | bytes 1572864 | tf_op jit(solution)/shard_map/convert_element_type | solution.py:237
  (35 shorter events, 0.4 us)
Async XLA Ops:
  0.0 4.1 %copy-start = (bf16[1,2,128,1024]{3,2,1,0:T(8,128)(2,1)S(1)}, bf16[1,2,128,1024]{3,2,1,0:T(8,128)(2,1)}, u32[]{:S(2)}) copy-start(bf16[1,2,128,1024]{3,2,1,0:T(8,128)(2,1)} %param.4) | copy-start | bytes 1572868
  1.0 10.2 %collective-permute-start = (bf16[1,128,1024]{2,1,0:T(8,128)(2,1)S(1)}, bf16[1,128,1024]{2,1,0:T(8,128)(2,1)S(1)}, u32[]{:S(2)}, u32[]{:S(2)}) collective-permute-start(bf16[1,128,1024]{2,1,0:T(8,128)(2,1)S(1)} %slice_bitcast_fusion), channel_id=1, source_target_pairs={{0,4},{4,0},{8,12},{12,8},{16,20},{20,16},{24,28},{28,24},{1,5},{5... | collective-permute-start | bytes 786440 | tf_op jit(solution)/shard_map/ppermute | solution.py:210
  4.1 11.8 %collective-permute-start.2 = (bf16[1,128,512]{2,1,0:T(8,128)(2,1)S(1)}, bf16[1,128,512]{2,1,0:T(8,128)(2,1)S(1)}, u32[]{:S(2)}, u32[]{:S(2)}) collective-permute-start(bf16[1,128,512]{2,1,0:T(8,128)(2,1)S(1)} %get-tuple-element.17), channel_id=1, source_target_pairs={{0,4},{4,0},{8,12},{12,8},{16,20},{20,16},{24,28},{28,24},{1,5},{5... | collective-permute-start | bytes 393224 | tf_op jit(solution)/shard_map/ppermute | solution.py:210
  4.2 15.2 %collective-permute-start.1 = (bf16[1,128,512]{2,1,0:T(8,128)(2,1)S(1)}, bf16[1,128,512]{2,1,0:T(8,128)(2,1)S(1)}, u32[]{:S(2)}, u32[]{:S(2)}) collective-permute-start(bf16[1,128,512]{2,1,0:T(8,128)(2,1)S(1)} %get-tuple-element.18), channel_id=1, source_target_pairs={{0,4},{4,0},{8,12},{12,8},{16,20},{20,16},{24,28},{28,24},{1,5},{5... | collective-permute-start | bytes 393224 | tf_op jit(solution)/shard_map/ppermute | solution.py:210
  9.1 23.5 %collective-permute-start.6 = (bf16[288,256]{1,0:T(8,128)(2,1)}, bf16[288,256]{1,0:T(8,128)(2,1)S(1)}, u32[]{:S(2)}, u32[]{:S(2)}) collective-permute-start(bf16[288,256]{1,0:T(8,128)(2,1)} %get-tuple-element.14), channel_id=1, source_target_pairs={{0,1},{1,0},{2,3},{3,2},{4,5},{5,4},{6,7},{7,6},{8,9},{9,8},{10,11... | collective-permute-start | bytes 442376 | tf_op jit(solution)/shard_map/ppermute | solution.py:188
  11.3 12.6 %copy-start.1 = (bf16[1,128,1024]{2,1,0:T(8,128)(2,1)}, bf16[1,128,1024]{2,1,0:T(8,128)(2,1)S(1)}, u32[]{:S(2)}) copy-start(bf16[1,128,1024]{2,1,0:T(8,128)(2,1)S(1)} %collective-permute-done) | copy-start | bytes 786436
  11.3 16.8 %collective-permute-start.3 = (bf16[1,128,1024]{2,1,0:T(8,128)(2,1)S(1)}, bf16[1,128,1024]{2,1,0:T(8,128)(2,1)S(1)}, u32[]{:S(2)}, u32[]{:S(2)}) collective-permute-start(bf16[1,128,1024]{2,1,0:T(8,128)(2,1)S(1)} %collective-permute-done), channel_id=1, source_target_pairs={{0,8},{8,16},{16,24},{12,4},{20,12},{28,20},{1,9},{9,17},{17,25},{... | collective-permute-start | bytes 786440 | tf_op jit(solution)/shard_map/ppermute | solution.py:211
  15.3 0.7 %copy-start.10 = (s32[2,27]{1,0:T(2,128)S(1)}, s32[2,27]{1,0:T(2,128)}, u32[]{:S(2)}) copy-start(s32[2,27]{1,0:T(2,128)} %param.7) | copy-start | bytes 652
  15.9 7.0 %copy-start.11 = (s32[2,27]{1,0:T(2,128)S(1)}, s32[2,27]{1,0:T(2,128)}, u32[]{:S(2)}) copy-start(s32[2,27]{1,0:T(2,128)} %param.6) | copy-start | bytes 652
  15.9 8.0 %copy-start.3 = (bf16[1,128,512]{2,1,0:T(8,128)(2,1)}, bf16[1,128,512]{2,1,0:T(8,128)(2,1)S(1)}, u32[]{:S(2)}) copy-start(bf16[1,128,512]{2,1,0:T(8,128)(2,1)S(1)} %collective-permute-done.2) | copy-start | bytes 393220
  16.0 12.1 %collective-permute-start.5 = (bf16[1,128,512]{2,1,0:T(8,128)(2,1)S(1)}, bf16[1,128,512]{2,1,0:T(8,128)(2,1)S(1)}, u32[]{:S(2)}, u32[]{:S(2)}) collective-permute-start(bf16[1,128,512]{2,1,0:T(8,128)(2,1)S(1)} %collective-permute-done.2), channel_id=1, source_target_pairs={{0,8},{8,16},{16,24},{12,4},{20,12},{28,20},{1,9},{9,17},{17,25},{... | collective-permute-start | bytes 393224 | tf_op jit(solution)/shard_map/ppermute | solution.py:211
  19.4 4.5 %copy-start.4 = (bf16[1,128,512]{2,1,0:T(8,128)(2,1)}, bf16[1,128,512]{2,1,0:T(8,128)(2,1)S(1)}, u32[]{:S(2)}) copy-start(bf16[1,128,512]{2,1,0:T(8,128)(2,1)S(1)} %collective-permute-done.1) | copy-start | bytes 393220
  19.5 8.6 %collective-permute-start.4 = (bf16[1,128,512]{2,1,0:T(8,128)(2,1)S(1)}, bf16[1,128,512]{2,1,0:T(8,128)(2,1)S(1)}, u32[]{:S(2)}, u32[]{:S(2)}) collective-permute-start(bf16[1,128,512]{2,1,0:T(8,128)(2,1)S(1)} %collective-permute-done.1), channel_id=1, source_target_pairs={{0,8},{8,16},{16,24},{12,4},{20,12},{28,20},{1,9},{9,17},{17,25},{... | collective-permute-start | bytes 393224 | tf_op jit(solution)/shard_map/ppermute | solution.py:211
  26.6 6.1 %collective-permute-start.7 = (bf16[272,256]{1,0:T(8,128)(2,1)}, bf16[272,256]{1,0:T(8,128)(2,1)S(1)}, u32[]{:S(2)}, u32[]{:S(2)}) collective-permute-start(bf16[272,256]{1,0:T(8,128)(2,1)} %get-tuple-element.15), channel_id=1, source_target_pairs={{0,1},{1,0},{2,3},{3,2},{4,5},{5,4},{6,7},{7,6},{8,9},{9,8},{10,11... | collective-permute-start | bytes 417800 | tf_op jit(solution)/shard_map/ppermute | solution.py:188
  28.1 0.6 %copy-start.5 = (bf16[1,128,512]{2,1,0:T(8,128)(2,1)}, bf16[1,128,512]{2,1,0:T(8,128)(2,1)S(1)}, u32[]{:S(2)}) copy-start(bf16[1,128,512]{2,1,0:T(8,128)(2,1)S(1)} %collective-permute-done.5) | copy-start | bytes 393220
  28.1 0.7 %copy-start.6 = (bf16[1,128,512]{2,1,0:T(8,128)(2,1)}, bf16[1,128,512]{2,1,0:T(8,128)(2,1)S(1)}, u32[]{:S(2)}) copy-start(bf16[1,128,512]{2,1,0:T(8,128)(2,1)S(1)} %collective-permute-done.4) | copy-start | bytes 393220
  28.1 0.8 %copy-start.2 = (bf16[1,128,1024]{2,1,0:T(8,128)(2,1)}, bf16[1,128,1024]{2,1,0:T(8,128)(2,1)S(1)}, u32[]{:S(2)}) copy-start(bf16[1,128,1024]{2,1,0:T(8,128)(2,1)S(1)} %collective-permute-done.3) | copy-start | bytes 786436
  31.5 5.3 %collective-permute-start.8 = (bf16[272,256]{1,0:T(8,128)(2,1)}, bf16[272,256]{1,0:T(8,128)(2,1)S(1)}, u32[]{:S(2)}, u32[]{:S(2)}) collective-permute-start(bf16[272,256]{1,0:T(8,128)(2,1)} %get-tuple-element.16), channel_id=1, source_target_pairs={{0,1},{1,0},{2,3},{3,2},{4,5},{5,4},{6,7},{7,6},{8,9},{9,8},{10,11... | collective-permute-start | bytes 417800 | tf_op jit(solution)/shard_map/ppermute | solution.py:188
  32.6 4.1 %copy-start.7 = (bf16[288,256]{1,0:T(8,128)(2,1)}, bf16[288,256]{1,0:T(8,128)(2,1)S(1)}, u32[]{:S(2)}) copy-start(bf16[288,256]{1,0:T(8,128)(2,1)S(1)} %collective-permute-done.6.refs_3_) | copy-start | bytes 442372
  32.6 4.1 %copy-start.8 = (bf16[272,256]{1,0:T(8,128)(2,1)}, bf16[272,256]{1,0:T(8,128)(2,1)S(1)}, u32[]{:S(2)}) copy-start(bf16[272,256]{1,0:T(8,128)(2,1)S(1)} %collective-permute-done.7.refs_4_) | copy-start | bytes 417796
  36.8 0.6 %copy-start.9 = (bf16[272,256]{1,0:T(8,128)(2,1)}, bf16[272,256]{1,0:T(8,128)(2,1)S(1)}, u32[]{:S(2)}) copy-start(bf16[272,256]{1,0:T(8,128)(2,1)S(1)} %collective-permute-done.8.refs_5_) | copy-start | bytes 417796
  41.6 2.1 %collective-permute-start.9 = (bf16[256,1024]{1,0:T(8,128)(2,1)}, bf16[256,1024]{1,0:T(8,128)(2,1)S(1)}, u32[]{:S(2)}, u32[]{:S(2)}) collective-permute-start(bf16[256,1024]{1,0:T(8,128)(2,1)} %shard_map.49), channel_id=1, source_target_pairs={{0,2},{2,0},{1,3},{3,1},{4,6},{6,4},{5,7},{7,5},{8,10},{10,8},{9,1... | collective-permute-start | bytes 1572872 | tf_op jit(solution)/shard_map/ppermute | solution.py:188

commit v2 on v1

--- a/solution.py
+++ b/solution.py
@@ -8,6 +8,7 @@
 from jax.sharding import PartitionSpec as P
 
 ITERS = 3
+SCOPE = 16 * 2**20
 PIECES = ((0, 1, 0, 8), (1, 1, 0, 4), (1, 1, 4, 4))
 
 
@@ -16,6 +17,10 @@
     for first, count, start, length in PIECES if eighths else ((0, blocks, 0, 8),):
         parts.append((first, count, start * times // 8, length * times // 8))
     return parts
+
+
+def near_core(value):
+    return pltpu.with_memory_space_constraint(value, pltpu.VMEM)
 
 
 def rows_dot(left, right):
@@ -70,10 +75,11 @@
     return pl.pallas_call(
         functools.partial(cross_body, parts, blocks, width, with_rows),
         out_shape=(
-            jax.ShapeDtypeStruct((rows + 8 * extra, lanes), jnp.float32),
-            jax.ShapeDtypeStruct((rows + 16 * extra, lanes), jnp.bfloat16),
+            pltpu.VMEM((rows + 8 * extra, lanes), jnp.float32),
+            pltpu.VMEM((rows + 16 * extra, lanes), jnp.bfloat16),
         ),
-    )(tmpl, *pieces)
+        compiler_params=pltpu.CompilerParams(vmem_limit_bytes=SCOPE),
+    )(*map(near_core, (tmpl, *pieces)))
 
 
 def plan_body(parts, blocks, width, n_others, count_ref, goal_ref, *refs):
@@ -172,14 +178,15 @@
     arrays = [*local, *(r for group in received for r in group), *(d for g in data for d in g)]
     return pl.pallas_call(
         functools.partial(plan_body, parts, blocks, width, len(received[0])),
-        out_shape=jax.ShapeDtypeStruct((rows, data[0][0].shape[1]), jnp.bfloat16),
+        out_shape=pltpu.VMEM((rows, data[0][0].shape[1]), jnp.bfloat16),
         in_specs=[smem, smem] + [vmem] * len(arrays),
         out_specs=vmem,
         scratch_shapes=[
             pltpu.VMEM((rows, 3 * rows), jnp.float32),
             pltpu.VMEM((rows, 3 * rows), jnp.bfloat16),
         ],
-    )(counts, goal, *arrays)
+        compiler_params=pltpu.CompilerParams(vmem_limit_bytes=SCOPE),
+    )(counts, goal, *map(near_core, arrays))
 
 
 def others(value, axis):

time: 46.1 us -> 36.9 us (0.80)
  Pallas kernels: 12.3 us -> 4.46 us
  local copies, waits for them, and re-layouts: 3.78 us -> 1.78 us
  other arithmetic: 2.97 us -> 1.34 us
  waiting for transfers between devices: 6.89 us -> 8.16 us
  starting transfers between devices: 19.6 us -> 20.8 us
    pallas_call x3, Pallas kernels: 8.16 us -> 2.32 us  [cross_call(): pl.pallas_call(functools.partial(cross_body, parts, blocks, width, with_r...]
    pallas_call x1, Pallas kernels: 4.15 us -> 2.14 us  [plan_call(): pl.pallas_call(functools.partial(plan_body, parts, blocks, width, len(rec...]
    ppermute x3, waiting for transfers between devices: 0.65 us -> 2.55 us  [on_device(): near.append(lax.ppermute(piece, 'slab', pairs))]
    unnamed x24 -> x8, local copies, waits for them, and re-layouts: 2.04 us -> 0.61 us
    ppermute x4, starting transfers between devices: 3.52 us -> 4.59 us  [others(): lax.ppermute(value, axis, [(i, (i + shift) % count) for i in range(count)])]
    convert_element_type x1, other arithmetic: 2.03 us -> 0.99 us  [on_device(): return (total / subjects).astype(jnp.bfloat16).reshape(template.shape)]
    ppermute x4, waiting for transfers between devices: 6.23 us -> 5.6 us  [others(): lax.ppermute(value, axis, [(i, (i + shift) % count) for i in range(count)])]
    div x1, other arithmetic: 0.6 us -> 0.01 us  [on_device(): goal = 1.0 / (width * jnp.sum(used, axis=1))]
  transfers between devices with their start and end apart: 10 -> 10, of which waited for: 3 -> 4; matrix products, arithmetic and copies ran while one was open for 4% -> 1% of each run, Pallas kernels for 18% -> 6%
where the time goes in v2:
time: 36.9 us; the launch traced here: 36.7 us
  starting transfers between devices  20.8 us (56%)
  waiting for transfers between devices  8.16 us (22%)
  Pallas kernels  4.46 us (12%)
  local copies, waits for them, and re-layouts  1.78 us (5%)
  other arithmetic  1.34 us (4%)
    ppermute x3, starting transfers between devices, on_device(): far.append(lax.ppermute(near[-1], 'slab', onward))  11.1 us
    ppermute x4, waiting for transfers between devices, others(): lax.ppermute(value, axis, [(i, (i + shift) % count) for i in range(count)])  5.6 us
    ppermute x3, starting transfers between devices, on_device(): near.append(lax.ppermute(piece, 'slab', pairs))  5.15 us
    ppermute x4, starting transfers between devices, others(): lax.ppermute(value, axis, [(i, (i + shift) % count) for i in range(count)])  4.59 us
    ppermute x3, waiting for transfers between devices, on_device(): near.append(lax.ppermute(piece, 'slab', pairs))  2.55 us
    pallas_call x3, Pallas kernels, cross_call(): pl.pallas_call(functools.partial(cross_body, parts, blocks, width, with_r...  2.32 us
    pallas_call x1, Pallas kernels, plan_call(): pl.pallas_call(functools.partial(plan_body, parts, blocks, width, len(rec...  2.14 us
    slice x2, local copies, waits for them, and re-layouts, on_device(): piece = data[first:first + count, :, start:start + length]  1.07 us
  transfers between devices with their start and end apart: 10, of which 4 were waited for; matrix products, arithmetic and copies ran while one was open for 1% of the time, Pallas kernels for 6%

profile of v2, /device:TPU:0, one launch (start us, length us, event | category | flops | bytes accessed | tf_op | source)
XLA Modules:
  0.0 36.7 jit_solution(4340301441824481096)
XLA Ops:
  0.0 1.1 %slice_bitcast_fusion = bf16[1,128,1024]{2,1,0:T(8,128)(2,1)S(1)} fusion(bf16[1,2,128,1024]{3,2,1,0:T(8,128)(2,1)} %param.4), kind=kLoop, calls=%fused_computation.1 | loop fusion | bytes 524288 | tf_op jit(solution)/shard_map/slice | solution.py:216
  1.1 3.1 %collective-permute-start = (bf16[1,128,1024]{2,1,0:T(8,128)(2,1)S(1)}, bf16[1,128,1024]{2,1,0:T(8,128)(2,1)S(1)}, u32[]{:S(2)}, u32[]{:S(2)}) collective-permute-start(bf16[1,128,1024]{2,1,0:T(8,128)(2,1)S(1)} %slice_bitcast_fusion), channel_id=1, source_target_pairs={{0,4},{4,0},{8,12},{12,8},{16,20},{20,16},{24,28},{28,24},{1,5},{5... | collective-permute-start | bytes 786440 | tf_op jit(solution)/shard_map/ppermute | solution.py:217
  4.1 0.1 collective-permute-start.2
  4.2 2.0 %collective-permute-start.1 = (bf16[1,128,512]{2,1,0:T(8,128)(2,1)S(1)}, bf16[1,128,512]{2,1,0:T(8,128)(2,1)S(1)}, u32[]{:S(2)}, u32[]{:S(2)}) collective-permute-start(bf16[1,128,512]{2,1,0:T(8,128)(2,1)S(1)} %get-tuple-element.18), channel_id=1, source_target_pairs={{0,4},{4,0},{8,12},{12,8},{16,20},{20,16},{24,28},{28,24},{1,5},{5... | collective-permute-start | bytes 393224 | tf_op jit(solution)/shard_map/ppermute | solution.py:217
  6.2 0.9 %shard_map.46 = (f32[272,256]{1,0:T(8,128)S(1)}, bf16[288,256]{1,0:T(8,128)(2,1)S(1)}) custom-call(bf16[256,1024]{1,0:T(8,128)(2,1)S(1)} %bitcast.12, bf16[256,1024]{1,0:T(8,128)(2,1)S(1)} %bitcast.16), custom_call_target="tpu_custom_call" | custom-call | tf_op jit(solution)/shard_map/pallas_call | solution.py:75
  7.2 1.6 %collective-permute-start.6 = (bf16[288,256]{1,0:T(8,128)(2,1)S(1)}, bf16[288,256]{1,0:T(8,128)(2,1)S(1)}, u32[]{:S(2)}, u32[]{:S(2)}) collective-permute-start(bf16[288,256]{1,0:T(8,128)(2,1)S(1)} %get-tuple-element.14), channel_id=1, source_target_pairs={{0,1},{1,0},{2,3},{3,2},{4,5},{5,4},{6,7},{7,6},{8,9},{9,8},{10,11... | collective-permute-start | bytes 442376 | tf_op jit(solution)/shard_map/ppermute | solution.py:195
  8.7 2.5 %collective-permute-done = bf16[1,128,1024]{2,1,0:T(8,128)(2,1)S(1)} collective-permute-done((bf16[1,128,1024]{2,1,0:T(8,128)(2,1)S(1)}, bf16[1,128,1024]{2,1,0:T(8,128)(2,1)S(1)}, u32[]{:S(2)}, u32[]{:S(2)}) %collective-permute-start) | collective-permute-done | bytes 262176 | tf_op jit(solution)/shard_map/ppermute | solution.py:217
  11.3 4.0 %collective-permute-start.3 = (bf16[1,128,1024]{2,1,0:T(8,128)(2,1)S(1)}, bf16[1,128,1024]{2,1,0:T(8,128)(2,1)S(1)}, u32[]{:S(2)}, u32[]{:S(2)}) collective-permute-start(bf16[1,128,1024]{2,1,0:T(8,128)(2,1)S(1)} %collective-permute-done), channel_id=1, source_target_pairs={{0,8},{8,16},{16,24},{12,4},{20,12},{28,20},{1,9},{9,17},{17,25},{... | collective-permute-start | bytes 786440 | tf_op jit(solution)/shard_map/ppermute | solution.py:218
  15.3 0.1 pad_add_fusion
  15.4 0.6 %copy-done.2 = s32[2,27]{1,0:T(2,128)S(1)} copy-done((s32[2,27]{1,0:T(2,128)S(1)}, s32[2,27]{1,0:T(2,128)}, u32[]{:S(2)}) %copy-start.2) | copy-done | bytes 240
  16.0 3.6 %collective-permute-start.5 = (bf16[1,128,512]{2,1,0:T(8,128)(2,1)S(1)}, bf16[1,128,512]{2,1,0:T(8,128)(2,1)S(1)}, u32[]{:S(2)}, u32[]{:S(2)}) collective-permute-start(bf16[1,128,512]{2,1,0:T(8,128)(2,1)S(1)} %collective-permute-done.2), channel_id=1, source_target_pairs={{0,8},{8,16},{16,24},{12,4},{20,12},{28,20},{1,9},{9,17},{17,25},{... | collective-permute-start | bytes 393224 | tf_op jit(solution)/shard_map/ppermute | solution.py:218
  19.6 3.5 %collective-permute-start.4 = (bf16[1,128,512]{2,1,0:T(8,128)(2,1)S(1)}, bf16[1,128,512]{2,1,0:T(8,128)(2,1)S(1)}, u32[]{:S(2)}, u32[]{:S(2)}) collective-permute-start(bf16[1,128,512]{2,1,0:T(8,128)(2,1)S(1)} %collective-permute-done.1), channel_id=1, source_target_pairs={{0,8},{8,16},{16,24},{12,4},{20,12},{28,20},{1,9},{9,17},{17,25},{... | collective-permute-start | bytes 393224 | tf_op jit(solution)/shard_map/ppermute | solution.py:218
  23.1 0.2 fusion
  23.2 0.1 copy.5.count_ref
  23.3 0.1 convert_reduce_fusion
  23.5 0.7 %shard_map.47 = (f32[264,256]{1,0:T(8,128)S(1)}, bf16[272,256]{1,0:T(8,128)(2,1)S(1)}) custom-call(bf16[256,1024]{1,0:T(8,128)(2,1)S(1)} %bitcast.13, bf16[128,1024]{1,0:T(8,128)(2,1)S(1)} %bitcast.18, bf16[128,512]{1,0:T(8,128)(2,1)S(1)} %bitcast.24, bf16[128,512]{1,0:T(8,128)(2,1)S(1)} %bitcast.22), custom_call_target="tpu_custom_call" | custom-call | tf_op jit(solution)/shard_map/pallas_call | solution.py:75
  24.2 1.6 %collective-permute-start.7 = (bf16[272,256]{1,0:T(8,128)(2,1)S(1)}, bf16[272,256]{1,0:T(8,128)(2,1)S(1)}, u32[]{:S(2)}, u32[]{:S(2)}) collective-permute-start(bf16[272,256]{1,0:T(8,128)(2,1)S(1)} %get-tuple-element.15), channel_id=1, source_target_pairs={{0,1},{1,0},{2,3},{3,2},{4,5},{5,4},{6,7},{7,6},{8,9},{9,8},{10,11... | collective-permute-start | bytes 417800 | tf_op jit(solution)/shard_map/ppermute | solution.py:195
  25.7 0.7 %shard_map.48 = (f32[264,256]{1,0:T(8,128)S(1)}, bf16[272,256]{1,0:T(8,128)(2,1)S(1)}) custom-call(bf16[256,1024]{1,0:T(8,128)(2,1)S(1)} %bitcast.14, bf16[128,1024]{1,0:T(8,128)(2,1)S(1)} %bitcast.20, bf16[128,512]{1,0:T(8,128)(2,1)S(1)} %bitcast.28, bf16[128,512]{1,0:T(8,128)(2,1)S(1)} %bitcast.26), custom_call_target="tpu_custom_call" | custom-call | tf_op jit(solution)/shard_map/pallas_call | solution.py:75
  26.4 1.4 %collective-permute-start.8 = (bf16[272,256]{1,0:T(8,128)(2,1)S(1)}, bf16[272,256]{1,0:T(8,128)(2,1)S(1)}, u32[]{:S(2)}, u32[]{:S(2)}) collective-permute-start(bf16[272,256]{1,0:T(8,128)(2,1)S(1)} %get-tuple-element.16), channel_id=1, source_target_pairs={{0,1},{1,0},{2,3},{3,2},{4,5},{5,4},{6,7},{7,6},{8,9},{9,8},{10,11... | collective-permute-start | bytes 417800 | tf_op jit(solution)/shard_map/ppermute | solution.py:195
  27.8 1.9 %collective-permute-done.7.refs_4_ = bf16[272,256]{1,0:T(8,128)(2,1)S(1)} collective-permute-done((bf16[272,256]{1,0:T(8,128)(2,1)S(1)}, bf16[272,256]{1,0:T(8,128)(2,1)S(1)}, u32[]{:S(2)}, u32[]{:S(2)}) %collective-permute-start.7) | collective-permute-done | bytes 139296 | tf_op jit(solution)/shard_map/ppermute | solution.py:195
  29.7 1.8 %collective-permute-done.8.refs_5_ = bf16[272,256]{1,0:T(8,128)(2,1)S(1)} collective-permute-done((bf16[272,256]{1,0:T(8,128)(2,1)S(1)}, bf16[272,256]{1,0:T(8,128)(2,1)S(1)}, u32[]{:S(2)}, u32[]{:S(2)}) %collective-permute-start.8) | collective-permute-done | bytes 139296 | tf_op jit(solution)/shard_map/ppermute | solution.py:195
  31.5 2.1 %shard_map.49 = bf16[256,1024]{1,0:T(8,128)(2,1)S(1)} custom-call(f32[2,6]{1,0:T(2,128)S(1)} %copy.5.count_ref, f32[2]{0:T(128)S(1)} %multiply_divide_fusion.goal_ref, f32[272,256]{1,0:T(8,128)S(1)} %get-tuple-element.11.refs_0_, f32[264,256]{1,0:T(8,128)S(1)} %get-tuple-element.12.refs_1_, f32[264,256]{1,0:T(8,128)S(1)} %get-tuple-element.13.refs_2_, ...), custom_call_target="tpu_custom_call" | custom-call | tf_op jit(solution)/shard_map/pallas_call | solution.py:179
  33.8 1.9 %collective-permute-done.9 = bf16[256,1024]{1,0:T(8,128)(2,1)S(1)} collective-permute-done((bf16[256,1024]{1,0:T(8,128)(2,1)S(1)}, bf16[256,1024]{1,0:T(8,128)(2,1)S(1)}, u32[]{:S(2)}, u32[]{:S(2)}) %collective-permute-start.9) | collective-permute-done | bytes 524320 | tf_op jit(solution)/shard_map/ppermute | solution.py:195
  35.7 1.0 %multiply_convert_fusion = bf16[256,1024]{1,0:T(8,128)(2,1)} fusion(bf16[256,1024]{1,0:T(8,128)(2,1)S(1)} %collective-permute-done.9, bf16[256,1024]{1,0:T(8,128)(2,1)S(1)} %shard_map.49), kind=kLoop, calls=%fused_computation | loop fusion | flops 1310720 | bytes 1572864 | tf_op jit(solution)/shard_map/convert_element_type | solution.py:244
  (19 shorter events, 0.1 us)
Async XLA Ops:
  0.0 4.1 %copy-start.1 = (bf16[1,2,128,1024]{3,2,1,0:T(8,128)(2,1)S(1)}, bf16[1,2,128,1024]{3,2,1,0:T(8,128)(2,1)}, u32[]{:S(2)}) copy-start(bf16[1,2,128,1024]{3,2,1,0:T(8,128)(2,1)} %param.4) | copy-start | bytes 1572868
  0.0 6.2 %copy-start = (bf16[2,128,1024]{2,1,0:T(8,128)(2,1)S(1)}, bf16[2,128,1024]{2,1,0:T(8,128)(2,1)}, u32[]{:S(2)}) copy-start(bf16[2,128,1024]{2,1,0:T(8,128)(2,1)} %param.5) | copy-start | bytes 1572868
  1.1 10.2 %collective-permute-start = (bf16[1,128,1024]{2,1,0:T(8,128)(2,1)S(1)}, bf16[1,128,1024]{2,1,0:T(8,128)(2,1)S(1)}, u32[]{:S(2)}, u32[]{:S(2)}) collective-permute-start(bf16[1,128,1024]{2,1,0:T(8,128)(2,1)S(1)} %slice_bitcast_fusion), channel_id=1, source_target_pairs={{0,4},{4,0},{8,12},{12,8},{16,20},{20,16},{24,28},{28,24},{1,5},{5... | collective-permute-start | bytes 786440 | tf_op jit(solution)/shard_map/ppermute | solution.py:217
  4.1 11.8 %collective-permute-start.2 = (bf16[1,128,512]{2,1,0:T(8,128)(2,1)S(1)}, bf16[1,128,512]{2,1,0:T(8,128)(2,1)S(1)}, u32[]{:S(2)}, u32[]{:S(2)}) collective-permute-start(bf16[1,128,512]{2,1,0:T(8,128)(2,1)S(1)} %get-tuple-element.17), channel_id=1, source_target_pairs={{0,4},{4,0},{8,12},{12,8},{16,20},{20,16},{24,28},{28,24},{1,5},{5... | collective-permute-start | bytes 393224 | tf_op jit(solution)/shard_map/ppermute | solution.py:217
  4.2 15.3 %collective-permute-start.1 = (bf16[1,128,512]{2,1,0:T(8,128)(2,1)S(1)}, bf16[1,128,512]{2,1,0:T(8,128)(2,1)S(1)}, u32[]{:S(2)}, u32[]{:S(2)}) collective-permute-start(bf16[1,128,512]{2,1,0:T(8,128)(2,1)S(1)} %get-tuple-element.18), channel_id=1, source_target_pairs={{0,4},{4,0},{8,12},{12,8},{16,20},{20,16},{24,28},{28,24},{1,5},{5... | collective-permute-start | bytes 393224 | tf_op jit(solution)/shard_map/ppermute | solution.py:217
  7.2 20.7 %collective-permute-start.6 = (bf16[288,256]{1,0:T(8,128)(2,1)S(1)}, bf16[288,256]{1,0:T(8,128)(2,1)S(1)}, u32[]{:S(2)}, u32[]{:S(2)}) collective-permute-start(bf16[288,256]{1,0:T(8,128)(2,1)S(1)} %get-tuple-element.14), channel_id=1, source_target_pairs={{0,1},{1,0},{2,3},{3,2},{4,5},{5,4},{6,7},{7,6},{8,9},{9,8},{10,11... | collective-permute-start | bytes 442376 | tf_op jit(solution)/shard_map/ppermute | solution.py:195
  11.3 14.4 %collective-permute-start.3 = (bf16[1,128,1024]{2,1,0:T(8,128)(2,1)S(1)}, bf16[1,128,1024]{2,1,0:T(8,128)(2,1)S(1)}, u32[]{:S(2)}, u32[]{:S(2)}) collective-permute-start(bf16[1,128,1024]{2,1,0:T(8,128)(2,1)S(1)} %collective-permute-done), channel_id=1, source_target_pairs={{0,8},{8,16},{16,24},{12,4},{20,12},{28,20},{1,9},{9,17},{17,25},{... | collective-permute-start | bytes 786440 | tf_op jit(solution)/shard_map/ppermute | solution.py:218
  15.3 0.7 %copy-start.2 = (s32[2,27]{1,0:T(2,128)S(1)}, s32[2,27]{1,0:T(2,128)}, u32[]{:S(2)}) copy-start(s32[2,27]{1,0:T(2,128)} %param.7) | copy-start | bytes 652
  16.0 7.1 %copy-start.3 = (s32[2,27]{1,0:T(2,128)S(1)}, s32[2,27]{1,0:T(2,128)}, u32[]{:S(2)}) copy-start(s32[2,27]{1,0:T(2,128)} %param.6) | copy-start | bytes 652
  16.0 9.8 %collective-permute-start.5 = (bf16[1,128,512]{2,1,0:T(8,128)(2,1)S(1)}, bf16[1,128,512]{2,1,0:T(8,128)(2,1)S(1)}, u32[]{:S(2)}, u32[]{:S(2)}) collective-permute-start(bf16[1,128,512]{2,1,0:T(8,128)(2,1)S(1)} %collective-permute-done.2), channel_id=1, source_target_pairs={{0,8},{8,16},{16,24},{12,4},{20,12},{28,20},{1,9},{9,17},{17,25},{... | collective-permute-start | bytes 393224 | tf_op jit(solution)/shard_map/ppermute | solution.py:218
  19.6 6.1 %collective-permute-start.4 = (bf16[1,128,512]{2,1,0:T(8,128)(2,1)S(1)}, bf16[1,128,512]{2,1,0:T(8,128)(2,1)S(1)}, u32[]{:S(2)}, u32[]{:S(2)}) collective-permute-start(bf16[1,128,512]{2,1,0:T(8,128)(2,1)S(1)} %collective-permute-done.1), channel_id=1, source_target_pairs={{0,8},{8,16},{16,24},{12,4},{20,12},{28,20},{1,9},{9,17},{17,25},{... | collective-permute-start | bytes 393224 | tf_op jit(solution)/shard_map/ppermute | solution.py:218
  24.2 5.6 %collective-permute-start.7 = (bf16[272,256]{1,0:T(8,128)(2,1)S(1)}, bf16[272,256]{1,0:T(8,128)(2,1)S(1)}, u32[]{:S(2)}, u32[]{:S(2)}) collective-permute-start(bf16[272,256]{1,0:T(8,128)(2,1)S(1)} %get-tuple-element.15), channel_id=1, source_target_pairs={{0,1},{1,0},{2,3},{3,2},{4,5},{5,4},{6,7},{7,6},{8,9},{9,8},{10,11... | collective-permute-start | bytes 417800 | tf_op jit(solution)/shard_map/ppermute | solution.py:195
  26.4 5.1 %collective-permute-start.8 = (bf16[272,256]{1,0:T(8,128)(2,1)S(1)}, bf16[272,256]{1,0:T(8,128)(2,1)S(1)}, u32[]{:S(2)}, u32[]{:S(2)}) collective-permute-start(bf16[272,256]{1,0:T(8,128)(2,1)S(1)} %get-tuple-element.16), channel_id=1, source_target_pairs={{0,1},{1,0},{2,3},{3,2},{4,5},{5,4},{6,7},{7,6},{8,9},{9,8},{10,11... | collective-permute-start | bytes 417800 | tf_op jit(solution)/shard_map/ppermute | solution.py:195
  33.7 2.0 %collective-permute-start.9 = (bf16[256,1024]{1,0:T(8,128)(2,1)S(1)}, bf16[256,1024]{1,0:T(8,128)(2,1)S(1)}, u32[]{:S(2)}, u32[]{:S(2)}) collective-permute-start(bf16[256,1024]{1,0:T(8,128)(2,1)S(1)} %shard_map.49), channel_id=1, source_target_pairs={{0,2},{2,0},{1,3},{3,1},{4,6},{6,4},{5,7},{7,5},{8,10},{10,8},{9,1... | collective-permute-start | bytes 1572872 | tf_op jit(solution)/shard_map/ppermute | solution.py:195
